TPU v7x, 256 devices: a whole 4x4x8 slice. The times are simulated.
256 devices in a mesh: gz: 32 (over z, y), ex: 8 (over x, core).
Axes of the slice: x: 4, y: 4, z: 8, core: 2. Of those that a mesh axis runs over, the one named last changes fastest.
Arguments:
- tokens: bfloat16 [256, 128, 1152], P('ex', 'gz'), may hold values from -12 to 12
- modulation: float32 [6, 1152], replicated, may hold values from -3 to 3
- w_qkv: bfloat16 [3, 1152, 1152], P(None, None, 'ex'), may hold values from -0.1875 to 0.1875
- w_proj: bfloat16 [1152, 1152], P('ex'), may hold values from -0.1875 to 0.1875
- phase: int32 [16], replicated, may hold values from 0 to 3
- routes: int32 [8, 32, 128, 2], P('ex', 'gz'), may hold values from 0 to 7, all different within a row; in each aligned block of 128 rows (0 to 127, 128 to 255, ..., all dimensions but the last counted through in order) at most 64 rows name the same one
- gates: float32 [8, 32, 128, 2], P('ex', 'gz'), may hold values from 0.2 to 1
- w_in: bfloat16 [8, 4608, 1152], P('ex', 'gz'), may hold values from -0.1875 to 0.1875
- w_out: bfloat16 [8, 4608, 1152], P('ex', 'gz'), may hold values from -0.09375 to 0.09375
Outputs:
- updated: bfloat16 [256, 128, 1152], P('ex', 'gz')
Inputs may be any that keep to these rules, and one draw needn't show every extreme that they name: Among the rows of one device no expert is named by more than 64 routes, and in every draw some expert is named by exactly 64 routes of one device.
All inputs are finite; a program needn't handle non-finite values.
Results may differ from a plain program's by a relative error of at most 0.0049.
Values may be sent and summed in bfloat16 or wider, within the bound.
A program may use at most 128 MiB of HBM per device.

v0:
```python
import math

import jax
import jax.numpy as jnp
from jax import lax
from jax.sharding import PartitionSpec as P

HEAD_DIM = 72
TILE = 16
WZ = 4


EPS = 1e-06


def padded(cells, sides, width):
    for axis, dim in sides:
        count = lax.axis_size(axis)
        ends = count - 1
        head = lax.slice_in_dim(cells, 0, width, axis=dim)
        tail = lax.slice_in_dim(cells, cells.shape[dim] - width, cells.shape[dim], axis=dim)
        cells = jnp.concatenate(
            [
                lax.ppermute(tail, axis, [(i, (i + 1) % count) for i in range(ends)]),
                cells,
                lax.ppermute(head, axis, [((i + 1) % count, i) for i in range(ends)]),
            ],
            axis=dim,
        )
    return cells


def layer_norm(values):
    center = jnp.mean(values, axis=-1, keepdims=True)
    centered = values - center
    spread = jnp.mean(centered * centered, axis=-1, keepdims=True)
    return centered / jnp.sqrt(spread + EPS)


def head_norm(values):
    return values / jnp.sqrt(jnp.mean(values * values, axis=-1, keepdims=True) + EPS)


def modulate(values, shift, scale):
    return layer_norm(values) * (1.0 + scale) + shift


def window_mix(queries, key_value, phase, base_plane, total_planes):
    columns, planes, local_width = queries.shape
    extent = key_value.shape[1]
    margin = (extent - planes) // 2
    tile_count = columns // TILE
    heads_here = local_width // HEAD_DIM
    query_rows = queries.reshape(tile_count, TILE * planes, heads_here, HEAD_DIM)
    key_rows = key_value[:, :, 0].reshape(tile_count, TILE * extent, heads_here, HEAD_DIM)
    value_rows = key_value[:, :, 1].reshape(tile_count, TILE * extent, heads_here, HEAD_DIM)
    scores = jnp.einsum(
        "tqhd,tkhd->thqk", query_rows, key_rows, preferred_element_type=jnp.float32
    ) * (1.0 / math.sqrt(HEAD_DIM))
    query_plane = base_plane + jnp.arange(planes, dtype=jnp.int32)
    key_plane = base_plane - margin + jnp.arange(extent, dtype=jnp.int32)
    offsets = phase.reshape(tile_count, 1)
    query_window = jnp.broadcast_to(
        ((query_plane[None, :] + offsets) // WZ)[:, None, :], (tile_count, TILE, planes)
    ).reshape(tile_count, TILE * planes)
    key_window = jnp.broadcast_to(
        ((key_plane[None, :] + offsets) // WZ)[:, None, :], (tile_count, TILE, extent)
    ).reshape(tile_count, TILE * extent)
    key_inside = (key_plane >= 0) & (key_plane < total_planes)
    key_valid = jnp.broadcast_to(key_inside[None, None, :], (tile_count, TILE, extent)).reshape(
        tile_count, TILE * extent
    )
    allowed = (query_window[:, :, None] == key_window[:, None, :]) & key_valid[:, None, :]
    weights_raw = jnp.where(allowed[:, None], jnp.exp(scores), 0.0)
    shares = (weights_raw / jnp.sum(weights_raw, axis=-1, keepdims=True)).astype(jnp.bfloat16)
    mixture = jnp.einsum(
        "thqk,tkhd->tqhd", shares, value_rows, preferred_element_type=jnp.float32
    ).astype(jnp.bfloat16)
    return mixture.reshape(columns, planes, local_width)


def per_device(tokens, modulation, w_qkv, w_proj, phase, routes, gates, w_in, w_out):
    columns_here, planes, features = tokens.shape
    local_width = w_qkv.shape[2]
    gz_count = lax.axis_size("gz")
    expert_count = lax.axis_size("ex")
    base_plane = lax.axis_index("gz") * planes
    total_planes = planes * gz_count
    halo_width = WZ - 1
    normed = modulate(tokens.astype(jnp.float32), modulation[0], modulation[1]).astype(jnp.bfloat16)
    pieces = lax.all_gather(normed, "ex", axis=0, tiled=True)
    row_count = pieces.shape[0]
    flattened = pieces.reshape(row_count * planes, features)
    projected = jnp.einsum("nc,icd->nid", flattened, w_qkv, preferred_element_type=jnp.float32)
    projected = projected.reshape(row_count * planes, 3, local_width // HEAD_DIM, HEAD_DIM)
    settled = jnp.concatenate([head_norm(projected[:, 0:2]), projected[:, 2:3]], axis=1)
    triple = settled.astype(jnp.bfloat16).reshape(row_count, planes, 3, local_width)
    key_value = padded(triple[:, :, 1:3], (("gz", 1),), halo_width)
    mixture = window_mix(triple[:, :, 0], key_value, phase, base_plane, total_planes)
    row_count = columns_here * lax.axis_size("ex")
    picked = mixture
    product = jnp.dot(
        picked.reshape(row_count * planes, local_width), w_proj, preferred_element_type=jnp.float32
    )
    attended = lax.psum_scatter(
        product.reshape(row_count, planes, features).astype(jnp.bfloat16),
        "ex",
        scatter_dimension=0,
        tiled=True,
    ).astype(jnp.float32)
    residual = tokens.astype(jnp.float32) + modulation[2] * attended
    moe_in = (
        modulate(residual, modulation[3], modulation[4])
        .astype(jnp.bfloat16)
        .reshape(columns_here * planes, features)
    )
    token_count = moe_in.shape[0]
    route_count = routes.shape[3]
    capacity = 2 * token_count * route_count // expert_count
    slot_total = expert_count * capacity
    route_flat = routes.reshape(token_count * route_count)
    onehot = (route_flat[:, None] == jnp.arange(expert_count, dtype=jnp.int32)[None, :]).astype(
        jnp.int32
    )
    ranking = jnp.cumsum(onehot, axis=0) - 1
    slot_index = jnp.sum(ranking * onehot, axis=1)
    target = route_flat * capacity + slot_index
    owner = jnp.arange(token_count * route_count, dtype=jnp.int32) // route_count
    slot_table = jnp.full((slot_total,), token_count, jnp.int32).at[target].set(owner)
    padded_in = jnp.concatenate([moe_in, jnp.zeros((1, features), jnp.bfloat16)], axis=0)
    outgoing = padded_in[slot_table].reshape(expert_count, capacity, features)
    contract = (((1,), (1,)), ((), ()))
    arrived = lax.all_to_all(outgoing, "ex", split_axis=0, concat_axis=0, tiled=True)
    work_rows = arrived.reshape(slot_total, features)
    hidden = jax.nn.gelu(
        lax.dot_general(
            work_rows,
            lax.all_gather(w_in, "gz", axis=1, tiled=True)[0],
            contract,
            preferred_element_type=jnp.float32,
        ),
        approximate=True,
    ).astype(jnp.bfloat16)
    folded = jnp.dot(
        hidden,
        lax.all_gather(w_out, "gz", axis=1, tiled=True)[0],
        preferred_element_type=jnp.float32,
    )
    expert_out = folded.astype(jnp.bfloat16)
    returned = lax.all_to_all(
        expert_out.reshape(expert_count, capacity, features),
        "ex",
        split_axis=0,
        concat_axis=0,
        tiled=True,
    )
    picked = (
        returned.reshape(slot_total, features)[target]
        .astype(jnp.float32)
        .reshape(token_count, route_count, features)
    )
    moe_sum = jnp.sum(picked * gates.reshape(token_count, route_count)[:, :, None], axis=1)
    updated = residual + modulation[5] * moe_sum.reshape(columns_here, planes, features)
    return updated.astype(jnp.bfloat16)


def solution(mesh):
    return jax.shard_map(
        per_device,
        mesh=mesh,
        in_specs=(
            P("ex", "gz", None),
            P(),
            P(None, None, "ex"),
            P("ex", None),
            P(),
            P("ex", "gz", None, None),
            P("ex", "gz", None, None),
            P("ex", "gz", None),
            P("ex", "gz", None),
        ),
        out_specs=P("ex", "gz", None),
        check_vma=False,
    )
```

profile of v0, /device:TPU:34, one launch (start us, length us, event | category | flops | bytes accessed | tf_op | source)
XLA Modules:
  0.0 369.1 jit_solution(14565762191397265147)
XLA Ops:
  10.8 1.9 fusion.38
  14.6 28.1 %all-gather.4.cloned.1.call-done = bf16[256,4,1152]{2,0,1:T(8,128)(2,1)} async-done(((bf16[32,4,1152]{2,0,1:T(8,128)(2,1)}), bf16[256,4,1152]{2,0,1:T(8,128)(2,1)}) %all-gather.4.cloned.1.call-update) | async-done | bytes 2359312 | tf_op jit(solution)/shard_map/all_gather | solution.py:91
  42.7 3.5 copy.33
  46.2 2.1 reshape.264
  48.4 3.0 fusion.17
  56.2 3.4 collective-permute-start
  59.6 4.7 %collective-permute-start.1 = (bf16[256,3,2,144]{0,3,2,1:T(8,128)(2,1)S(1)}, bf16[256,3,2,144]{0,3,2,1:T(8,128)(2,1)}, u32[]{:S(2)}, u32[]{:S(2)}) collective-permute-start(bf16[256,3,2,144]{0,3,2,1:T(8,128)(2,1)S(1)} %get-tuple-element.14), channel_id=1, source_target_pairs={{8,0},{16,8},{24,16},{32,24},{40,32},{48,40},{56,48},{64,56},{72,6... | collective-permute-start | bytes 1327112 | tf_op jit(solution)/shard_map/ppermute | solution.py:26
  65.3 3.1 slice_reduce_fusion
  69.7 3.0 collective-permute-done
  76.0 3.9 %copy.40 = bf16[256,10,1,144]{3,1,0,2:T(8,128)(2,1)S(1)} copy(bf16[256,10,1,144]{0,3,2,1:T(8,128)(2,1)} %get-tuple-element.11) | data formatting | bytes 1474560 | tf_op jit(solution)/shard_map/slice | solution.py:55
  79.8 1.9 reshape_squeeze.11
  81.7 3.0 copy.38
  84.8 1.9 reshape_squeeze.9
  86.7 2.5 fusion.19
  90.9 2.3 convolution_convert_fusion
  97.5 33.3 %reduce-scatter.2.cloned.1.call-done = bf16[32,4,1152]{2,0,1:T(8,128)(2,1)} async-done(((bf16[256,4,1152]{2,0,1:T(8,128)(2,1)}), bf16[32,4,1152]{2,0,1:T(8,128)(2,1)}) %reduce-scatter.2.cloned.1.call-update) | async-done | bytes 294928 | tf_op jit(solution)/shard_map/reduce_scatter | solution.py:105
  134.6 2.1 gather_fusion
  136.7 22.9 %all_to_all.10 = bf16[8,64,1152]{2,1,0:T(8,128)(2,1)} all-to-all(bf16[8,64,1152]{2,1,0:T(8,128)(2,1)S(1)} %bitcast.53), channel_id=1, replica_groups=mesh['gz'=32,'ex'=8] {'ex'}, dimensions={0} | all-to-all | bytes 2359296 | tf_op jit(solution)/shard_map/all_to_all | solution.py:133
  159.6 47.4 %all-gather.6.cloned.1.call-done = bf16[1,4608,1152]{2,1,0:T(8,128)(2,1)} async-done(((bf16[1,144,1152]{2,1,0:T(8,128)(2,1)}), bf16[1,4608,1152]{2,1,0:T(8,128)(2,1)}) %all-gather.6.cloned.1.call-update) | async-done | bytes 10616848 | tf_op jit(solution)/shard_map/all_gather | solution.py:138
  207.0 108.5 %all-gather.8.cloned.1.call-done = bf16[1,4608,1152]{2,1,0:T(8,128)(2,1)} async-done(((bf16[1,144,1152]{2,1,0:T(8,128)(2,1)}), bf16[1,4608,1152]{2,1,0:T(8,128)(2,1)}) %all-gather.8.cloned.1.call-update) | async-done | bytes 10616848 | tf_op jit(solution)/shard_map/all_gather | solution.py:146
  315.5 20.8 %fusion.14 = bf16[512,1152]{1,0:T(8,128)(2,1)} fusion(bf16[1,4608,1152]{2,1,0:T(8,128)(2,1)} %all-gather.8.cloned.1.call-done, bf16[512,1152]{1,0:T(8,128)(2,1)} %bitcast.55, bf16[1,4608,1152]{2,1,0:T(8,128)(2,1)} %all-gather.6.cloned.1.call-done), kind=kOutput, calls=%fused_computation.17 | convolution fusion | flops 10893459456 | bytes 23592960 | tf_op jit(solution)/shard_map/dot_general | solution.py:144
  336.3 4.9 %all-to-all-start.1 = ((bf16[8,64,1152]{2,1,0:T(8,128)(2,1)}), bf16[8,64,1152]{2,1,0:T(8,128)(2,1)S(1)}, u32[]{:S(2)}, u32[]{:S(2)}) async-start(bf16[8,64,1152]{2,1,0:T(8,128)(2,1)} %bitcast.54), calls=%async_computation.2 | async-start | bytes 2359296 | tf_op jit(solution)/shard_map/all_to_all | solution.py:150
  341.4 15.8 %all-to-all-done.1 = bf16[8,64,1152]{2,1,0:T(8,128)(2,1)S(1)} async-done(((bf16[8,64,1152]{2,1,0:T(8,128)(2,1)}), bf16[8,64,1152]{2,1,0:T(8,128)(2,1)S(1)}, u32[]{:S(2)}, u32[]{:S(2)}) %all-to-all-start.1) | async-done | bytes 1179680 | tf_op jit(solution)/shard_map/all_to_all | solution.py:150
  359.0 1.4 multiply_reduce_fusion
  (96 shorter events, 28.3 us)
Async XLA Ops:
  7.4 41.0 %copy-start = (bf16[3,1152,144]{1,2,0:T(8,128)(2,1)S(1)}, bf16[3,1152,144]{1,2,0:T(8,128)(2,1)}, u32[]{:S(2)}) copy-start(bf16[3,1152,144]{1,2,0:T(8,128)(2,1)} %param.11) | copy-start | bytes 2985988
  7.4 35.4 %all-gather.4.cloned.1.call-start = ((), (), s32[]{:S(2)}) async-start(), calls=%async_computation.3 | async-start | bytes 2654208 | tf_op jit(solution)/shard_map/all_gather | solution.py:91
  12.7 118.1 %reduce-scatter.2.cloned.1.call-start = ((), (), s32[]{:S(2)}) async-start(), calls=%async_computation.4 | async-start | bytes 2654208 | tf_op jit(solution)/shard_map/reduce_scatter | solution.py:105
  56.2 16.4 %collective-permute-start = (bf16[256,3,2,144]{0,3,2,1:T(8,128)(2,1)S(1)}, bf16[256,3,2,144]{0,3,2,1:T(8,128)(2,1)}, u32[]{:S(2)}, u32[]{:S(2)}) collective-permute-start(bf16[256,3,2,144]{0,3,2,1:T(8,128)(2,1)S(1)} %get-tuple-element.13), channel_id=1, source_target_pairs={{0,8},{8,16},{16,24},{24,32},{32,40},{40,48},{48,56},{56,64},{64,7... | collective-permute-start | bytes 1327112 | tf_op jit(solution)/shard_map/ppermute | solution.py:24
  59.6 14.1 %collective-permute-start.1 = (bf16[256,3,2,144]{0,3,2,1:T(8,128)(2,1)S(1)}, bf16[256,3,2,144]{0,3,2,1:T(8,128)(2,1)}, u32[]{:S(2)}, u32[]{:S(2)}) collective-permute-start(bf16[256,3,2,144]{0,3,2,1:T(8,128)(2,1)S(1)} %get-tuple-element.14), channel_id=1, source_target_pairs={{8,0},{16,8},{24,16},{32,24},{40,32},{48,40},{56,48},{64,56},{72,6... | collective-permute-start | bytes 1327112 | tf_op jit(solution)/shard_map/ppermute | solution.py:26
  84.8 1.9 copy-start.5
  84.8 1.9 copy-start.7
  86.7 2.5 copy-start.4
  90.0 1.0 copy-start.6
  93.2 1.2 copy-start.8
  93.2 37.6 %copy-start.2 = (bf16[32,4,1152]{2,1,0:T(4,128)(2,1)S(1)}, bf16[32,4,1152]{2,1,0:T(4,128)(2,1)}, u32[]{:S(2)}) copy-start(bf16[32,4,1152]{2,1,0:T(4,128)(2,1)} %param.9) | copy-start | bytes 884740
  93.3 113.7 %all-gather.6.cloned.1.call-start = ((), (), s32[]{:S(2)}) async-start(), calls=%async_computation.5 | async-start | bytes 10948608 | tf_op jit(solution)/shard_map/all_gather | solution.py:138
  93.9 221.7 %all-gather.8.cloned.1.call-start = ((), (), s32[]{:S(2)}) async-start(), calls=%async_computation.6 | async-start | bytes 10948608 | tf_op jit(solution)/shard_map/all_gather | solution.py:146
  336.3 4.9 %copy-start.9 = (f32[1,1,128,2]{2,3,1,0:T(2,128)S(1)}, f32[1,1,128,2]{2,3,1,0:T(2,128)}, u32[]{:S(2)}) copy-start(f32[1,1,128,2]{2,3,1,0:T(2,128)} %param.15) | copy-start | bytes 3076
  336.3 20.8 %all-to-all-start.1 = ((bf16[8,64,1152]{2,1,0:T(8,128)(2,1)}), bf16[8,64,1152]{2,1,0:T(8,128)(2,1)S(1)}, u32[]{:S(2)}, u32[]{:S(2)}) async-start(bf16[8,64,1152]{2,1,0:T(8,128)(2,1)} %bitcast.54), calls=%async_computation.2 | async-start | bytes 2359296 | tf_op jit(solution)/shard_map/all_to_all | solution.py:150
  358.4 2.2 copy-start.3
  358.5 3.2 copy-start.1
Sparse Core Ops, SparseCore 0:
  12.8 29.8 all-gather.3
  93.4 37.3 reduce-scatter.1
Sparse Core Ops, SparseCore 1:
  96.3 110.6 all-gather.5
  209.5 106.0 all-gather.7
where the time goes:
time: 373 us; the launch traced here: 369 us
  waiting for transfers between devices  238 us (64%)
  local copies, waits for them, and re-layouts  34.8 us (9%)
  matrix products  29.4 us (8%)
  blocking collectives  22.9 us (6%)
  between operations  15.3 us (4%)
  other arithmetic  15.2 us (4%)
  starting transfers between devices  13.4 us (4%)
    all_gather x1, waiting for transfers between devices, per_device(): lax.all_gather(w_out, 'gz', axis=1, tiled=True)[0]  109 us
    all_gather x1, waiting for transfers between devices, per_device(): lax.all_gather(w_in, 'gz', axis=1, tiled=True)[0]  47.4 us
    reduce_scatter x1, waiting for transfers between devices, per_device(): lax.psum_scatter(product.reshape(row_count, planes, features).astype(jnp....  33.3 us
    all_gather x1, waiting for transfers between devices, per_device(): pieces = lax.all_gather(normed, 'ex', axis=0, tiled=True)  28.1 us
    all_to_all x1, blocking collectives, per_device(): lax.all_to_all(outgoing, 'ex', split_axis=0, concat_axis=0, tiled=True)  22.9 us
    dot_general x1, matrix products, per_device(): jnp.dot(hidden, lax.all_gather(w_out, 'gz', axis=1, tiled=True)[0], prefe...  20.8 us
    all_to_all x1, waiting for transfers between devices, per_device(): lax.all_to_all(expert_out.reshape(expert_count, capacity, features), 'ex'...  15.8 us
  transfers between devices with their start and end apart: 7, of which 7 were waited for; matrix products, arithmetic and copies ran while one was open for 4% of the time, Pallas kernels for 0%

commit v1 on v0

v1 whole, which is shorter than its diff:
```python
import functools
import math

import jax
import jax.numpy as jnp
from jax import lax
from jax.experimental import pallas as pl
from jax.experimental.pallas import tpu as pltpu
from jax.sharding import PartitionSpec as P

D = 1152
HEAD_DIM = 72
PAIR = 144
FF_HERE = 144
TOK = 128
CAP = 64
NZC = 8
NYC = 4
NEX = 8
RY = 64
RZ = 80
EPS = 1e-06
BF = jnp.bfloat16
F32 = jnp.float32
NT = (((1,), (1,)), ((), ()))
MESH = pl.DeviceIdType.MESH


def dot(a, b):
    return jnp.dot(a, b, preferred_element_type=F32)


def dot_nt(a, b):
    return lax.dot_general(a, b, NT, preferred_element_type=F32)


def modulate(values, shift, scale):
    centered = values - jnp.mean(values, axis=-1, keepdims=True)
    spread = jnp.mean(centered * centered, axis=-1, keepdims=True)
    return centered * lax.rsqrt(spread + EPS) * (1.0 + scale) + shift


def gelu(u):
    return 0.5 * u * (1.0 + jnp.tanh(0.7978845608 * (u + 0.044715 * (u * u * u))))


HALO = 0
YP = 2
YZ = 5
ZZ = 19
ZA = 26
ZB = 34
ZC = 42
XX = 50
DI = 58
RE = 65
NSEM = 72


def kernel(
    tok, mod, wqkv, wproj, phase, routes, gates, win, wout, out,
    buf_y, buf_z, buf_x, halo, normed, mask, att, picks, out_buf, in_buf, acc, back, ret,
    send, recv, local,
):
    g = lax.axis_index("gz")
    e = lax.axis_index("ex")
    z, y = g // NYC, g % NYC
    x, core = e // 2, e % 2
    sigma = 1 - 2 * core
    zp = ((z + sigma + NZC) % NZC) * NYC + y
    zm = ((z - sigma + NZC) % NZC) * NYC + y
    y1 = z * NYC + (y + 1) % NYC
    y2 = z * NYC + (y + 2) % NYC
    y3 = z * NYC + (y + 3) % NYC
    gp = (g + 1) % (NZC * NYC)
    gm = (g + NZC * NYC - 1) % (NZC * NYC)
    xp = ((x + 1) % 4) * 2 + core
    xm = ((x + 3) % 4) * 2 + core
    sib = x * 2 + 1 - core

    def remote(src, dst, number, axis, where):
        return pltpu.make_async_remote_copy(
            src_ref=src, dst_ref=dst, send_sem=send.at[number], recv_sem=recv.at[number],
            device_id={axis: where}, device_id_type=MESH,
        )

    def c_halo(k):
        return remote(tok, halo.at[k], HALO + k, "gz", (gp, gm)[k])

    def c_yp(k):
        own = buf_y.at[0, 0, :, 0:RY]
        dst = (buf_y.at[0, 0, :, RY : 2 * RY], buf_y.at[0, 1, :, 0:RY], buf_y.at[0, 1, :, RY : 2 * RY])[k]
        return remote(own, dst, YP + k, "gz", (y1, y3, y2)[k])

    def prior(t):
        return 0 if t <= 2 else t - 2

    def c_yz(t, h):
        return remote(
            buf_y.at[prior(t), h], buf_y.at[t, h], YZ + (t - 1) * 2 + h, "gz", zp if t % 2 else zm
        )

    def c_zz(t):
        return remote(buf_z.at[prior(t), 0], buf_z.at[t, 0], ZZ + t - 1, "gz", zp if t % 2 else zm)

    def c_za(t):
        return remote(buf_z.at[t, 0], buf_z.at[t, 1], ZA + t, "gz", y3 if t % 2 else y1)

    def c_zb(t):
        return remote(buf_z.at[t, 0], buf_z.at[t, 2], ZB + t, "gz", y1 if t % 2 else y3)

    def c_zc(t):
        return remote(buf_z.at[t, 1], buf_z.at[t, 3], ZC + t, "gz", y3 if t % 2 else y1)

    half = 2 * PAIR

    def c_x(k):
        src, dst, where = (
            (buf_x.at[0], buf_x.at[1], sib),
            (buf_x.at[0], buf_x.at[2], xp),
            (buf_x.at[0], buf_x.at[3], xm),
            (buf_x.at[2, 0:half], buf_x.at[6, 0:half], xp),
            (buf_x.at[3, half : 2 * half], buf_x.at[6, half : 2 * half], xm),
            (buf_x.at[2], buf_x.at[4], sib),
            (buf_x.at[3], buf_x.at[5], sib),
            (buf_x.at[6], buf_x.at[7], sib),
        )[k]
        return remote(src, dst, XX + k, "ex", where)

    def c_di(k):
        peer = (e + k) % NEX
        return remote(out_buf.at[peer], in_buf.at[e], DI + k - 1, "ex", peer)

    def c_re(k):
        peer = (e + k) % NEX
        return remote(back.at[peer], ret.at[e], RE + k - 1, "ex", peer)

    def ev_z(t):
        c_zz(t).wait_recv()
        if t <= 5:
            c_zz(t + 2).start()
        c_za(t).start()
        c_zb(t).start()

    def ev_r(t):
        c_za(t).wait_recv()
        c_zc(t).start()

    def ev_y0():
        for k in range(3):
            c_yp(k).wait_recv()
        for h in range(2):
            for t in (1, 2):
                c_yz(t, h).start()

    def ev_y(t, h):
        c_yz(t, h).wait_recv()
        if t <= 5:
            c_yz(t + 2, h).start()

    loads = [
        pltpu.make_async_copy(win.at[0:RY], buf_y.at[0, 0, 0, 0:RY], local.at[0]),
        pltpu.make_async_copy(wout.at[0:RY], buf_y.at[0, 0, 1, 0:RY], local.at[1]),
        pltpu.make_async_copy(win.at[RY:FF_HERE], buf_z.at[0, 0, 0], local.at[2]),
        pltpu.make_async_copy(wout.at[RY:FF_HERE], buf_z.at[0, 0, 1], local.at[3]),
        pltpu.make_async_copy(wproj, buf_x.at[0, 3 * PAIR : 4 * PAIR], local.at[4]),
    ]
    for load in loads:
        load.start()
    barrier = pltpu.get_barrier_semaphore()
    for where in (zp, zm, y1, y2, y3, gp, gm):
        pl.semaphore_signal(barrier, inc=1, device_id={"gz": where}, device_id_type=MESH)
    for k in range(1, NEX):
        pl.semaphore_signal(barrier, inc=1, device_id={"ex": (e + k) % NEX}, device_id_type=MESH)
    eye = (
        lax.broadcasted_iota(jnp.int32, (PAIR, PAIR), 0) == lax.broadcasted_iota(jnp.int32, (PAIR, PAIR), 1)
    ).astype(F32).astype(BF)
    for i in range(3):
        buf_x[0, i * PAIR : (i + 1) * PAIR, :] = dot_nt(eye, wqkv[i]).astype(BF)
    for load in loads:
        load.wait()
    pl.semaphore_wait(barrier, 7 + NEX - 1)

    for k in (2, 0, 1):
        c_yp(k).start()
    for k in range(2):
        c_halo(k).start()
    c_zz(1).start()
    c_zz(2).start()
    c_za(0).start()
    c_zb(0).start()
    for k in (1, 2, 0):
        c_x(k).start()

    normed[0:TOK, :] = modulate(tok[...].astype(F32), mod[0:1, :], mod[1:2, :]).astype(BF)
    phase0, phase1 = phase[2 * e], phase[2 * e + 1]
    rows = lax.broadcasted_iota(jnp.int32, (TOK, 3 * TOK), 0)
    cols = lax.broadcasted_iota(jnp.int32, (TOK, 3 * TOK), 1)
    row_tile = rows >> 6
    col_in = cols & (TOK - 1)
    block = cols >> 7
    offset = jnp.where(block == 2, 1, jnp.where(block == 1, -1, 0))
    shift = jnp.where(row_tile == 0, phase0, phase1)
    here = ((rows & 3) + shift) >> 2
    there = (((col_in & 3) + shift) >> 2) + offset
    plane_block = g + offset
    allowed = (
        (row_tile == (col_in >> 6)) & (here == there) & (plane_block >= 0) & (plane_block < NZC * NYC)
    )
    ones = jnp.where(allowed, 1.0, 0.0).astype(F32)
    mask[0:TOK, :] = ones
    mask[TOK : 2 * TOK, :] = ones
    for k in range(2):
        c_halo(k).wait_recv()
        normed[(k + 1) * TOK : (k + 2) * TOK, :] = modulate(
            halo[k].astype(F32), mod[0:1, :], mod[1:2, :]
        ).astype(BF)
    att[...] = jnp.zeros_like(att)

    def heads(j, carry):
        @pl.when(j == 1)
        def _():
            c_x(0).wait_recv()

        @pl.when(j == 2)
        def _():
            ev_z(1)
            ev_z(2)
            ev_y0()
            ev_z(3)
            ev_z(4)
            ev_r(0)
            ev_z(5)
            ev_z(6)
            c_x(1).wait_recv()
            c_x(3).start()
            c_x(5).start()

        @pl.when(j == 3)
        def _():
            c_x(2).wait_recv()
            c_x(4).start()
            c_x(6).start()
            ev_r(1)
            ev_z(7)

        @pl.when(j == 4)
        def _():
            c_x(5).wait_recv()

        @pl.when(j == 5)
        def _():
            c_x(6).wait_recv()
            ev_r(2)

        @pl.when(j == 6)
        def _():
            ev_y(1, 0)
            ev_y(2, 0)
            c_x(3).wait_recv()
            c_x(4).wait_recv()
            c_x(7).start()

        @pl.when(j == 7)
        def _():
            ev_r(3)
            c_x(7).wait_recv()

        low = lax.broadcasted_iota(jnp.int32, (TOK, PAIR), 1) < HEAD_DIM
        low3 = lax.broadcasted_iota(jnp.int32, (3 * TOK, PAIR), 1) < HEAD_DIM

        def normalise(values, first):
            squares = values * values
            one = jnp.sum(jnp.where(first, squares, 0.0), axis=-1, keepdims=True)
            two = jnp.sum(jnp.where(first, 0.0, squares), axis=-1, keepdims=True)
            return values * jnp.where(
                first,
                lax.rsqrt(one * (1.0 / HEAD_DIM) + EPS),
                lax.rsqrt(two * (1.0 / HEAD_DIM) + EPS),
            )

        query = normalise(dot_nt(normed[0:TOK, :], buf_x[j, 0:PAIR, :]), low)
        keys = normalise(dot_nt(normed[...], buf_x[j, PAIR : 2 * PAIR, :]), low3).astype(BF)
        values = dot_nt(normed[...], buf_x[j, 2 * PAIR : 3 * PAIR, :]).astype(BF)
        both = jnp.concatenate(
            [jnp.where(low, query, 0.0).astype(BF), jnp.where(low, 0.0, query).astype(BF)], axis=0
        )
        raw = jnp.exp(dot_nt(both, keys) * (1.0 / math.sqrt(HEAD_DIM))) * mask[...]
        shares = (raw / jnp.sum(raw, axis=-1, keepdims=True)).astype(BF)
        mixed = dot(shares, values)
        mixture = jnp.where(low, mixed[0:TOK], mixed[TOK : 2 * TOK]).astype(BF)
        att[...] += dot(mixture, buf_x[j, 3 * PAIR : 4 * PAIR, :])
        return carry

    lax.fori_loop(0, NEX, heads, 0)
    ev_y(1, 1)
    ev_y(2, 1)

    residual = tok[...].astype(F32) + mod[2:3, :] * att[...]
    att[...] = residual
    moe_in = modulate(residual, mod[3:4, :], mod[4:5, :]).astype(BF)
    lane = lax.broadcasted_iota(jnp.int32, (TOK, TOK), 1)
    r0, r1 = routes[:, 0:1], routes[:, 1:2]
    member = jnp.where((r0 == lane) | (r1 == lane), 1.0, 0.0).astype(BF)
    earlier = jnp.where(lax.broadcasted_iota(jnp.int32, (TOK, TOK), 0) > lane, 1.0, 0.0).astype(BF)
    spot = dot(earlier, member) + (lane * CAP).astype(F32)
    slots = lax.broadcasted_iota(jnp.int32, (TOK, NEX * CAP), 1).astype(F32)
    chosen = []
    for r in (r0, r1):
        target = jnp.sum(jnp.where(r == lane, spot, 0.0), axis=-1, keepdims=True)
        chosen.append(jnp.where(slots == target, 1.0, 0.0))
    picks[0] = chosen[0].astype(BF)
    picks[1] = chosen[1].astype(BF)
    table = jnp.transpose(chosen[0] + chosen[1]).astype(BF)
    out_buf[...] = dot(table, moe_in).astype(BF).reshape(NEX, CAP, D)
    ev_r(4)
    for k in (4, 5, 3, 2, 6, 1, 7):
        c_di(k).start()
    in_buf[e] = out_buf[e]
    acc[...] = jnp.zeros_like(acc)
    ev_y(3, 0)
    ev_y(4, 0)
    for k in range(1, NEX):
        c_di(k).wait_recv()

    def block_of(t, carry):
        @pl.when(t == 1)
        def _():
            ev_r(5)

        @pl.when(t == 2)
        def _():
            ev_y(3, 1)
            ev_y(4, 1)

        @pl.when(t == 4)
        def _():
            ev_r(6)
            ev_y(5, 0)
            ev_y(6, 0)

        @pl.when(t == 5)
        def _():
            ev_y(5, 1)
            ev_y(6, 1)
            ev_r(7)

        rows_in = in_buf[...].reshape(NEX * CAP, D)

        def part(first, second):
            hidden = gelu(dot_nt(rows_in, first)).astype(BF)
            acc[...] += dot(hidden, second)

        remote(buf_z.at[t, 0], buf_z.at[t, 2], ZB + t, "gz", y1).wait_recv()
        remote(buf_z.at[t, 1], buf_z.at[t, 3], ZC + t, "gz", y1).wait_recv()
        part(
            jnp.concatenate([buf_z[t, i, 0] for i in range(4)], axis=0),
            jnp.concatenate([buf_z[t, i, 1] for i in range(4)], axis=0),
        )

        @pl.when(t == 7)
        def _():
            ev_y(7, 0)
            ev_y(7, 1)

        part(
            jnp.concatenate([buf_y[t, i, 0] for i in range(2)], axis=0),
            jnp.concatenate([buf_y[t, i, 1] for i in range(2)], axis=0),
        )
        return carry

    lax.fori_loop(0, NZC, block_of, 0)

    back[...] = acc[...].astype(BF).reshape(NEX, CAP, D)
    for k in (4, 5, 3, 2, 6, 1, 7):
        c_re(k).start()
    ret[e] = back[e]
    for k in range(1, NEX):
        c_re(k).wait_recv()
    returned = ret[...].reshape(NEX * CAP, D)
    total = gates[:, 0:1] * dot(picks[0], returned) + gates[:, 1:2] * dot(picks[1], returned)
    out[...] = (att[...] + mod[5:6, :] * total).astype(BF)

    for k in range(2):
        c_halo(k).wait_send()
    for k in range(3):
        c_yp(k).wait_send()
    for t in range(1, 8):
        for h in range(2):
            c_yz(t, h).wait_send()
        c_zz(t).wait_send()
    for t in range(8):
        c_za(t).wait_send()
        c_zb(t).wait_send()
        c_zc(t).wait_send()
        c_x(t).wait_send()
    for k in range(1, NEX):
        c_di(k).wait_send()
        c_re(k).wait_send()


def per_device(tokens, modulation, w_qkv, w_proj, phase, routes, gates, w_in, w_out):
    columns, planes, _ = tokens.shape
    vmem = pl.BlockSpec(memory_space=pltpu.VMEM)
    anywhere = pl.BlockSpec(memory_space=pl.ANY)
    updated = pl.pallas_call(
        kernel,
        out_shape=jax.ShapeDtypeStruct((TOK, D), BF),
        in_specs=[
            vmem, vmem, vmem, anywhere, pl.BlockSpec(memory_space=pltpu.SMEM), vmem, vmem, anywhere, anywhere,
        ],
        out_specs=vmem,
        scratch_shapes=[
            pltpu.VMEM((NZC, 2, 2, 2 * RY, D), BF),
            pltpu.VMEM((NZC, NYC, 2, RZ, D), BF),
            pltpu.VMEM((NEX, 4 * PAIR, D), BF),
            pltpu.VMEM((2, TOK, D), BF),
            pltpu.VMEM((3 * TOK, D), BF),
            pltpu.VMEM((2 * TOK, 3 * TOK), F32),
            pltpu.VMEM((TOK, D), F32),
            pltpu.VMEM((2, TOK, NEX * CAP), BF),
            pltpu.VMEM((NEX, CAP, D), BF),
            pltpu.VMEM((NEX, CAP, D), BF),
            pltpu.VMEM((NEX * CAP, D), F32),
            pltpu.VMEM((NEX, CAP, D), BF),
            pltpu.VMEM((NEX, CAP, D), BF),
            pltpu.SemaphoreType.DMA((NSEM,)),
            pltpu.SemaphoreType.DMA((NSEM,)),
            pltpu.SemaphoreType.DMA((5,)),
        ],
        compiler_params=pltpu.CompilerParams(
            collective_id=0, has_side_effects=True, vmem_limit_bytes=60 * 1024 * 1024
        ),
        name="layer",
    )(
        tokens.reshape(TOK, D), modulation, w_qkv, w_proj, phase,
        routes.reshape(TOK, 2), gates.reshape(TOK, 2), w_in[0], w_out[0],
    )
    return updated.reshape(columns, planes, D)


def solution(mesh):
    return jax.shard_map(
        per_device,
        mesh=mesh,
        in_specs=(
            P("ex", "gz", None),
            P(),
            P(None, None, "ex"),
            P("ex", None),
            P(),
            P("ex", "gz", None, None),
            P("ex", "gz", None, None),
            P("ex", "gz", None),
            P("ex", "gz", None),
        ),
        out_specs=P("ex", "gz", None),
        check_vma=False,
    )
```

time: 373 us -> 182 us (0.49)
  waiting for transfers between devices: 238 us -> 0 us
  Pallas kernels: 0 us -> 172 us
  matrix products: 29.4 us -> 0 us
  local copies, waits for them, and re-layouts: 34.8 us -> 8.93 us
  blocking collectives: 22.9 us -> 0 us
  between operations: 15.3 us -> 0.01 us
  other arithmetic: 15.2 us -> 0 us
  starting transfers between devices: 13.4 us -> 0 us
    all_gather x3 -> x0, waiting for transfers between devices: 184 us -> none  [the longest x1 109 us: per_device(): lax.all_gather(w_out, 'gz', axis=1, tiled=True)[0]]
    pallas_call x0 -> x1, Pallas kernels: none -> 172 us  [per_device(): pl.pallas_call(kernel, out_shape=jax.ShapeDtypeStruct((TOK, D), BF), in_s...]
    reduce_scatter x1 -> x0, waiting for transfers between devices: 33.3 us -> none  [per_device(): lax.psum_scatter(product.reshape(row_count, planes, features).astype(jnp....]
    dot_general x5 -> x0, matrix products: 29.4 us -> none  [the longest x1 20.8 us: per_device(): jnp.dot(hidden, lax.all_gather(w_out, 'gz', axis=1, tiled=True)[0], prefe...]
    all_to_all x1 -> x0, blocking collectives: 22.9 us -> none  [per_device(): lax.all_to_all(outgoing, 'ex', split_axis=0, concat_axis=0, tiled=True)]
    all_to_all x1 -> x0, waiting for transfers between devices: 15.8 us -> none  [per_device(): lax.all_to_all(expert_out.reshape(expert_count, capacity, features), 'ex'...]
    slice x7 -> x0, local copies, waits for them, and re-layouts: 11.6 us -> none  [the longest x2 4.83 us: window_mix(): key_value[:, :, 0].reshape(tile_count, TILE * extent, heads_here, HEAD_DIM)]
    ppermute x2 -> x0, starting transfers between devices: 8.13 us -> none  [the longest x1 4.75 us: padded(): lax.ppermute(head, axis, [((i + 1) % count, i) for i in range(ends)])]
  transfers between devices with their start and end apart: 7 -> 0, of which waited for: 7 -> 0; matrix products, arithmetic and copies ran while one was open for 4% -> 0% of each run, Pallas kernels for 0% -> 0%
where the time goes in v1:
time: 182 us; the launch traced here: 181 us
  Pallas kernels  172 us (95%)
  local copies, waits for them, and re-layouts  8.93 us (5%)
    pallas_call x1, Pallas kernels, per_device(): pl.pallas_call(kernel, out_shape=jax.ShapeDtypeStruct((TOK, D), BF), in_s...  172 us
    unnamed x3, local copies, waits for them, and re-layouts  5.43 us

profile of v1, /device:TPU:34, one launch (start us, length us, event | category | flops | bytes accessed | tf_op | source)
XLA Modules:
  0.0 181.3 jit_solution(16032552611717429744)
XLA Ops:
  0.0 1.4 copy.10
  1.4 1.4 copy.11
  2.8 1.7 reshape.12.tok
  4.6 2.6 %copy.12.wqkv = bf16[3,1152,144]{2,1,0:T(8,128)(2,1)} copy(bf16[3,1152,144]{1,2,0:T(8,128)(2,1)} %param.11) | data formatting | bytes 1990656 | tf_op args[2]
  7.2 172.3 %layer.1 = bf16[128,1152]{1,0:T(8,128)(2,1)} custom-call(bf16[128,1152]{1,0:T(8,128)(2,1)} %reshape.12.tok, f32[6,1152]{1,0:T(8,128)} %mod.1, bf16[3,1152,144]{2,1,0:T(8,128)(2,1)} %copy.12.wqkv, bf16[144,1152]{1,0:T(8,128)(2,1)} %wproj.1, s32[16]{0:T(128)} %phase.1, s32[128,2]{1,0:T(8,128)} %bitcast.6, f32[128,2]{1,0:T(8,128)} %bitcast.7, ...), custom_call_target="tpu_custom_call" | custom-call | tf_op jit(solution)/shard_map/layer/pallas_call | solution.py:406
  179.5 1.8 reshape.15

commit v2 on v1

--- a/solution.py
+++ b/solution.py
@@ -59,7 +59,7 @@
 
 def kernel(
     tok, mod, wqkv, wproj, phase, routes, gates, win, wout, out,
-    buf_y, buf_z, buf_x, halo, normed, mask, att, picks, out_buf, in_buf, acc, back, ret,
+    buf_y, buf_z, buf_x, halo, normed, mask, att, picks, out_buf, in_buf, acc, back, ret, weights,
     send, recv, local,
 ):
     g = lax.axis_index("gz")
@@ -164,6 +164,8 @@
         pltpu.make_async_copy(win.at[RY:FF_HERE], buf_z.at[0, 0, 0], local.at[2]),
         pltpu.make_async_copy(wout.at[RY:FF_HERE], buf_z.at[0, 0, 1], local.at[3]),
         pltpu.make_async_copy(wproj, buf_x.at[0, 3 * PAIR : 4 * PAIR], local.at[4]),
+    ] + [
+        pltpu.make_async_copy(wqkv.at[i], buf_x.at[0, i * PAIR : (i + 1) * PAIR], local.at[5 + i]) for i in range(3)
     ]
     for load in loads:
         load.start()
@@ -172,11 +174,6 @@
         pl.semaphore_signal(barrier, inc=1, device_id={"gz": where}, device_id_type=MESH)
     for k in range(1, NEX):
         pl.semaphore_signal(barrier, inc=1, device_id={"ex": (e + k) % NEX}, device_id_type=MESH)
-    eye = (
-        lax.broadcasted_iota(jnp.int32, (PAIR, PAIR), 0) == lax.broadcasted_iota(jnp.int32, (PAIR, PAIR), 1)
-    ).astype(F32).astype(BF)
-    for i in range(3):
-        buf_x[0, i * PAIR : (i + 1) * PAIR, :] = dot_nt(eye, wqkv[i]).astype(BF)
     for load in loads:
         load.wait()
     pl.semaphore_wait(barrier, 7 + NEX - 1)
@@ -220,29 +217,25 @@
     def heads(j, carry):
         @pl.when(j == 1)
         def _():
-            c_x(0).wait_recv()
-
-        @pl.when(j == 2)
-        def _():
             ev_z(1)
             ev_z(2)
-            ev_y0()
+            c_x(0).wait_recv()
+
+        @pl.when(j == 2)
+        def _():
             ev_z(3)
             ev_z(4)
+            ev_y0()
+            ev_r(1)
             ev_r(0)
             ev_z(5)
             ev_z(6)
             c_x(1).wait_recv()
             c_x(3).start()
             c_x(5).start()
-
-        @pl.when(j == 3)
-        def _():
             c_x(2).wait_recv()
             c_x(4).start()
             c_x(6).start()
-            ev_r(1)
-            ev_z(7)
 
         @pl.when(j == 4)
         def _():
@@ -251,19 +244,19 @@
         @pl.when(j == 5)
         def _():
             c_x(6).wait_recv()
-            ev_r(2)
-
-        @pl.when(j == 6)
-        def _():
+            ev_r(3)
             ev_y(1, 0)
             ev_y(2, 0)
+
+        @pl.when(j == 6)
+        def _():
+            ev_r(2)
             c_x(3).wait_recv()
             c_x(4).wait_recv()
             c_x(7).start()
 
         @pl.when(j == 7)
         def _():
-            ev_r(3)
             c_x(7).wait_recv()
 
         low = lax.broadcasted_iota(jnp.int32, (TOK, PAIR), 1) < HEAD_DIM
@@ -300,57 +293,46 @@
     att[...] = residual
     moe_in = modulate(residual, mod[3:4, :], mod[4:5, :]).astype(BF)
     lane = lax.broadcasted_iota(jnp.int32, (TOK, TOK), 1)
-    r0, r1 = routes[:, 0:1], routes[:, 1:2]
-    member = jnp.where((r0 == lane) | (r1 == lane), 1.0, 0.0).astype(BF)
+    lane_f = lane.astype(F32)
+    r0, r1 = (jnp.transpose(jnp.broadcast_to(routes[r : r + 1, :].astype(F32), (TOK, TOK))) for r in range(2))
+    gate0, gate1 = (jnp.transpose(jnp.broadcast_to(gates[r : r + 1, :], (TOK, TOK))) for r in range(2))
+    weights[...] = jnp.where(lane == 0, gate0, gate1)
+    member = jnp.where((r0 == lane_f) | (r1 == lane_f), 1.0, 0.0).astype(BF)
     earlier = jnp.where(lax.broadcasted_iota(jnp.int32, (TOK, TOK), 0) > lane, 1.0, 0.0).astype(BF)
     spot = dot(earlier, member) + (lane * CAP).astype(F32)
     slots = lax.broadcasted_iota(jnp.int32, (TOK, NEX * CAP), 1).astype(F32)
     chosen = []
     for r in (r0, r1):
-        target = jnp.sum(jnp.where(r == lane, spot, 0.0), axis=-1, keepdims=True)
+        target = jnp.sum(jnp.where(r == lane_f, spot, 0.0), axis=-1, keepdims=True)
         chosen.append(jnp.where(slots == target, 1.0, 0.0))
     picks[0] = chosen[0].astype(BF)
     picks[1] = chosen[1].astype(BF)
     table = jnp.transpose(chosen[0] + chosen[1]).astype(BF)
     out_buf[...] = dot(table, moe_in).astype(BF).reshape(NEX, CAP, D)
-    ev_r(4)
     for k in (4, 5, 3, 2, 6, 1, 7):
         c_di(k).start()
+    ev_r(4)
     in_buf[e] = out_buf[e]
     acc[...] = jnp.zeros_like(acc)
-    ev_y(3, 0)
+    ev_z(7)
+    ev_r(5)
     ev_y(4, 0)
     for k in range(1, NEX):
         c_di(k).wait_recv()
 
-    def block_of(t, carry):
-        @pl.when(t == 1)
-        def _():
-            ev_r(5)
-
-        @pl.when(t == 2)
-        def _():
-            ev_y(3, 1)
-            ev_y(4, 1)
-
-        @pl.when(t == 4)
-        def _():
-            ev_r(6)
-            ev_y(5, 0)
-            ev_y(6, 0)
-
-        @pl.when(t == 5)
-        def _():
-            ev_y(5, 1)
-            ev_y(6, 1)
-            ev_r(7)
-
+    def block_of(s, carry):
         rows_in = in_buf[...].reshape(NEX * CAP, D)
 
         def part(first, second):
             hidden = gelu(dot_nt(rows_in, first)).astype(BF)
             acc[...] += dot(hidden, second)
 
+        @pl.when(s == 3)
+        def _():
+            ev_r(7)
+            ev_y(3, 1)
+
+        t = s + 1 - 2 * (s % 2)
         remote(buf_z.at[t, 0], buf_z.at[t, 2], ZB + t, "gz", y1).wait_recv()
         remote(buf_z.at[t, 1], buf_z.at[t, 3], ZC + t, "gz", y1).wait_recv()
         part(
@@ -358,14 +340,39 @@
             jnp.concatenate([buf_z[t, i, 1] for i in range(4)], axis=0),
         )
 
-        @pl.when(t == 7)
+        @pl.when(s == 0)
+        def _():
+            ev_y(3, 0)
+
+        @pl.when(s == 1)
+        def _():
+            ev_y(4, 1)
+
+        @pl.when(s == 2)
+        def _():
+            ev_r(6)
+
+        @pl.when(s == 3)
+        def _():
+            ev_y(6, 0)
+
+        @pl.when(s == 4)
+        def _():
+            ev_y(5, 0)
+
+        @pl.when(s == 5)
+        def _():
+            ev_y(6, 1)
+            ev_y(5, 1)
+
+        @pl.when(s == 7)
         def _():
             ev_y(7, 0)
             ev_y(7, 1)
 
         part(
-            jnp.concatenate([buf_y[t, i, 0] for i in range(2)], axis=0),
-            jnp.concatenate([buf_y[t, i, 1] for i in range(2)], axis=0),
+            jnp.concatenate([buf_y[s, i, 0] for i in range(2)], axis=0),
+            jnp.concatenate([buf_y[s, i, 1] for i in range(2)], axis=0),
         )
         return carry
 
@@ -378,7 +385,7 @@
     for k in range(1, NEX):
         c_re(k).wait_recv()
     returned = ret[...].reshape(NEX * CAP, D)
-    total = gates[:, 0:1] * dot(picks[0], returned) + gates[:, 1:2] * dot(picks[1], returned)
+    total = weights[:, 0:1] * dot(picks[0], returned) + weights[:, 1:2] * dot(picks[1], returned)
     out[...] = (att[...] + mod[5:6, :] * total).astype(BF)
 
     for k in range(2):
@@ -407,7 +414,7 @@
         kernel,
         out_shape=jax.ShapeDtypeStruct((TOK, D), BF),
         in_specs=[
-            vmem, vmem, vmem, anywhere, pl.BlockSpec(memory_space=pltpu.SMEM), vmem, vmem, anywhere, anywhere,
+            vmem, vmem, anywhere, anywhere, pl.BlockSpec(memory_space=pltpu.SMEM), vmem, vmem, anywhere, anywhere,
         ],
         out_specs=vmem,
         scratch_shapes=[
@@ -424,17 +431,18 @@
             pltpu.VMEM((NEX * CAP, D), F32),
             pltpu.VMEM((NEX, CAP, D), BF),
             pltpu.VMEM((NEX, CAP, D), BF),
+            pltpu.VMEM((TOK, TOK), F32),
             pltpu.SemaphoreType.DMA((NSEM,)),
             pltpu.SemaphoreType.DMA((NSEM,)),
-            pltpu.SemaphoreType.DMA((5,)),
+            pltpu.SemaphoreType.DMA((8,)),
         ],
         compiler_params=pltpu.CompilerParams(
             collective_id=0, has_side_effects=True, vmem_limit_bytes=60 * 1024 * 1024
         ),
         name="layer",
     )(
-        tokens.reshape(TOK, D), modulation, w_qkv, w_proj, phase,
-        routes.reshape(TOK, 2), gates.reshape(TOK, 2), w_in[0], w_out[0],
+        tokens.reshape(TOK, D), modulation, jnp.swapaxes(w_qkv, 1, 2), w_proj, phase,
+        routes.reshape(TOK, 2).T, gates.reshape(TOK, 2).T, w_in[0], w_out[0],
     )
     return updated.reshape(columns, planes, D)
 

time: 182 us -> 166 us (0.912)
  Pallas kernels: 172 us -> 162 us
  local copies, waits for them, and re-layouts: 8.93 us -> 3.5 us
    pallas_call x1, Pallas kernels: 172 us -> 162 us  [per_device(): pl.pallas_call(kernel, out_shape=jax.ShapeDtypeStruct((TOK, D), BF), in_s...]
    unnamed x3 -> x0, local copies, waits for them, and re-layouts: 5.43 us -> none
where the time goes in v2:
time: 166 us
  Pallas kernels  162 us (98%)
  local copies, waits for them, and re-layouts  3.5 us (2%)
    pallas_call x1, Pallas kernels, per_device(): pl.pallas_call(kernel, out_shape=jax.ShapeDtypeStruct((TOK, D), BF), in_s...  162 us

profile of v2, /device:TPU:34, one launch (start us, length us, event | category | flops | bytes accessed | tf_op | source)
XLA Modules:
  0.0 165.8 jit_solution(13452160938673716725)
XLA Ops:
  0.0 1.7 %reshape.12.tok = bf16[128,1152]{1,0:T(8,128)(2,1)} reshape(bf16[32,4,1152]{2,1,0:T(4,128)(2,1)} %param.9) | data formatting | bytes 589824 | tf_op jit(solution)/shard_map/reshape | solution.py:444
  1.7 162.3 %layer.1 = bf16[128,1152]{1,0:T(8,128)(2,1)} custom-call(bf16[128,1152]{1,0:T(8,128)(2,1)} %reshape.12.tok, f32[6,1152]{1,0:T(8,128)} %mod.1, bf16[3,144,1152]{2,1,0:T(8,128)(2,1)} %bitcast.9, bf16[144,1152]{1,0:T(8,128)(2,1)} %wproj.1, s32[16]{0:T(128)} %phase.1, s32[2,128]{1,0:T(2,128)} %bitcast.12, f32[2,128]{1,0:T(2,128)} %bitcast.13, ...), custom_call_target="tpu_custom_call" | custom-call | tf_op jit(solution)/shard_map/layer/pallas_call | solution.py:413
  164.1 1.8 %reshape.15 = bf16[32,4,1152]{2,1,0:T(4,128)(2,1)} reshape(bf16[128,1152]{1,0:T(8,128)(2,1)} %layer.1) | data formatting | bytes 589824 | tf_op jit(solution)/shard_map/reshape | solution.py:447

commit v3 on v2

--- a/solution.py
+++ b/solution.py
@@ -174,18 +174,20 @@
         pl.semaphore_signal(barrier, inc=1, device_id={"gz": where}, device_id_type=MESH)
     for k in range(1, NEX):
         pl.semaphore_signal(barrier, inc=1, device_id={"ex": (e + k) % NEX}, device_id_type=MESH)
-    for load in loads:
+    for load in loads[0:4]:
         load.wait()
     pl.semaphore_wait(barrier, 7 + NEX - 1)
 
+    c_zz(1).start()
+    c_zz(2).start()
     for k in (2, 0, 1):
         c_yp(k).start()
+    c_za(0).start()
+    c_zb(0).start()
     for k in range(2):
         c_halo(k).start()
-    c_zz(1).start()
-    c_zz(2).start()
-    c_za(0).start()
-    c_zb(0).start()
+    for load in loads[4:8]:
+        load.wait()
     for k in (1, 2, 0):
         c_x(k).start()
 
@@ -213,12 +215,12 @@
             halo[k].astype(F32), mod[0:1, :], mod[1:2, :]
         ).astype(BF)
     att[...] = jnp.zeros_like(att)
+    ev_z(1)
+    ev_z(2)
 
     def heads(j, carry):
         @pl.when(j == 1)
         def _():
-            ev_z(1)
-            ev_z(2)
             c_x(0).wait_recv()
 
         @pl.when(j == 2)

time: 166 us -> 169 us (1.018)
  Pallas kernels: 162 us -> 164 us
    pallas_call x1, Pallas kernels: 162 us -> 164 us  [per_device(): pl.pallas_call(kernel, out_shape=jax.ShapeDtypeStruct((TOK, D), BF), in_s...]
where the time goes in v3:
time: 169 us; the launch traced here: 168 us
  Pallas kernels  164 us (97%)
  local copies, waits for them, and re-layouts  3.5 us (2%)
    pallas_call x1, Pallas kernels, per_device(): pl.pallas_call(kernel, out_shape=jax.ShapeDtypeStruct((TOK, D), BF), in_s...  164 us

profile of v3, /device:TPU:34, one launch (start us, length us, event | category | flops | bytes accessed | tf_op | source)
XLA Modules:
  0.0 167.9 jit_solution(3517985653861463387)
XLA Ops:
  0.0 1.7 %reshape.12.tok = bf16[128,1152]{1,0:T(8,128)(2,1)} reshape(bf16[32,4,1152]{2,1,0:T(4,128)(2,1)} %param.9) | data formatting | bytes 589824 | tf_op jit(solution)/shard_map/reshape | solution.py:446
  1.7 164.4 %layer.1 = bf16[128,1152]{1,0:T(8,128)(2,1)} custom-call(bf16[128,1152]{1,0:T(8,128)(2,1)} %reshape.12.tok, f32[6,1152]{1,0:T(8,128)} %mod.1, bf16[3,144,1152]{2,1,0:T(8,128)(2,1)} %bitcast.9, bf16[144,1152]{1,0:T(8,128)(2,1)} %wproj.1, s32[16]{0:T(128)} %phase.1, s32[2,128]{1,0:T(2,128)} %bitcast.12, f32[2,128]{1,0:T(2,128)} %bitcast.13, ...), custom_call_target="tpu_custom_call" | custom-call | tf_op jit(solution)/shard_map/layer/pallas_call | solution.py:415
  166.1 1.8 %reshape.15 = bf16[32,4,1152]{2,1,0:T(4,128)(2,1)} reshape(bf16[128,1152]{1,0:T(8,128)(2,1)} %layer.1) | data formatting | bytes 589824 | tf_op jit(solution)/shard_map/reshape | solution.py:449
